TPU v7x, 32 devices: a whole 2x2x4 slice. The times are simulated.
32 devices in a mesh: radial: 8 (over y, x, core), mode: 4 (over z).
Axes of the slice: x: 2, y: 2, z: 4, core: 2. Of those that a mesh axis runs over, the one named last changes fastest.
Arguments:
- scalar_field: float32 [256, 64, 2, 384], P('radial', 'mode'), may hold values from -48 to 48
- radial_flow: float32 [256, 64, 2, 384], P('radial', 'mode'), may hold values from -6 to 6
- legendre: bfloat16 [64, 384, 768], P('mode'), may hold values from -0.3125 to 0.3125
- diffusivity: float32 [256], P('radial'), may hold values from 1000 to 100000
Outputs:
- field_new: float32 [256, 64, 2, 384], P('radial', 'mode')
All inputs are finite; a program needn't handle non-finite values.
Results may differ from a plain program's by a relative error of at most 0.0071.
Values may be sent and summed in bfloat16 or wider, within the bound.
A program may use at most 128 MiB of HBM per device.

v0:
```python
import math
import jax
import jax.numpy as jnp
from jax import lax
from jax.sharding import PartitionSpec as P

NLON = 1536


def prefix_2(value, axis, join, neutral, backward):
    count, mine = (lax.axis_size(axis), lax.axis_index(axis))
    pieces = jax.tree.map(lambda part: lax.all_gather(part, axis), value)
    if backward:
        pieces = jax.tree.map(lambda part: part[::-1], pieces)
        mine = count - 1 - mine
    total = jax.tree.map(
        lambda part, zero: jnp.full_like(part, 0) + jnp.asarray(zero, part.dtype), value, neutral
    )

    def hop(position, total):
        longer = join(total, jax.tree.map(lambda part: part[position], pieces))
        return jax.tree.map(lambda new, old: jnp.where(position < mine, new, old), longer, total)

    return lax.fori_loop(0, count - 1, hop, total)


def longitude_tables(orders, points):
    order_ids = jnp.arange(orders, dtype=jnp.int32)
    point_ids = jnp.arange(points, dtype=jnp.int32)
    phase = order_ids[:, None] * point_ids[None, :] % points
    angle = phase.astype(jnp.float32) * (2.0 * math.pi / points)
    cosine = jnp.cos(angle)
    sine_part = jnp.sin(angle)
    paired = jnp.stack([cosine, -sine_part], axis=1)
    synth_table = (paired / math.sqrt(orders)).astype(jnp.bfloat16)
    analysis_table = (paired * math.sqrt(2.0 / points)).astype(jnp.bfloat16)
    return (synth_table, analysis_table)


def normalized(matrix):
    largest = jnp.max(jnp.abs(matrix), axis=(0, 1))
    return matrix / largest


def combine_maps(earlier, later):
    return normalized(jnp.sum(later[:, :, None] * earlier[None, :, :], axis=1))


def combine_affine(earlier, later):
    return (later[0] + later[1][:, None, :] * earlier[0], later[1] * earlier[1])


def on_device(scalar_field, radial_flow, legendre, diffusivity):
    shells, ord_dev, halves, degrees = scalar_field.shape
    orders = ord_dev * lax.axis_size("mode")
    synth_table, analysis_table = longitude_tables(orders, NLON)
    field_lat = jnp.einsum(
        "rmcj,mjt->rmct",
        scalar_field.astype(jnp.bfloat16),
        legendre,
        preferred_element_type=jnp.float32,
    ).astype(jnp.bfloat16)
    flow_lat = jnp.einsum(
        "rmcj,mjt->rmct",
        radial_flow.astype(jnp.bfloat16),
        legendre,
        preferred_element_type=jnp.float32,
    ).astype(jnp.bfloat16)
    field_piece = lax.all_to_all(field_lat, "mode", split_axis=3, concat_axis=1, tiled=True)
    flow_piece = lax.all_to_all(flow_lat, "mode", split_axis=3, concat_axis=1, tiled=True)
    field_grid = jnp.einsum(
        "rmct,mcp->rtp", field_piece, synth_table, preferred_element_type=jnp.float32
    )
    flow_grid = jnp.einsum(
        "rmct,mcp->rtp", flow_piece, synth_table, preferred_element_type=jnp.float32
    )
    product = (field_grid * flow_grid).astype(jnp.bfloat16)
    modes_grid = jnp.einsum(
        "rtp,mcp->rmct", product, analysis_table, preferred_element_type=jnp.float32
    ).astype(jnp.bfloat16)
    spectral_back = lax.all_to_all(modes_grid, "mode", split_axis=1, concat_axis=3, tiled=True)
    forcing = jnp.einsum(
        "rmct,mjt->rmcj", spectral_back, legendre, preferred_element_type=jnp.float32
    )
    right_side = scalar_field + forcing
    radial_index = lax.axis_index("radial")
    nr_total = shells * lax.axis_size("radial")
    offset = nr_total * 7 // 13
    order_ids = (jnp.arange(ord_dev, dtype=jnp.int32) + lax.axis_index("mode") * ord_dev).astype(
        jnp.float32
    )
    degree = order_ids[:, None] + jnp.arange(degrees, dtype=jnp.float32)[None, :]
    angular = degree * (degree + 1.0)
    global_shells = radial_index * shells + jnp.arange(shells, dtype=jnp.int32)

    def coefficients(kappa_shell, shell_index):
        lower = jnp.where(shell_index > 0, -kappa_shell, 0.0)
        upper = jnp.where(shell_index < nr_total - 1, -kappa_shell, 0.0)
        radius = (offset + shell_index).astype(jnp.float32)
        diagonal = 1.0 + 2.0 * kappa_shell + kappa_shell * angular / (radius * radius)
        return (lower, upper, diagonal)

    identity = jnp.broadcast_to(
        jnp.eye(4, dtype=jnp.float32)[:, :, None, None], (4, 4, ord_dev, degrees)
    )

    def compose(composite, inputs):
        kappa_shell, source, shell_index = inputs
        lower, upper, diagonal = coefficients(kappa_shell, shell_index)
        new_rows = jnp.stack(
            [
                upper * composite[3],
                -lower * composite[1] + source[:, 0, :] * composite[3],
                -lower * composite[2] + source[:, 1, :] * composite[3],
                -lower * composite[0] + diagonal * composite[3],
            ]
        )
        return (normalized(new_rows), None)

    transfer, _ = lax.scan(compose, identity, (diffusivity, right_side, global_shells))
    prefix = prefix_2(transfer, "radial", combine_maps, identity, False)
    incoming = prefix[:, 3]
    ratio_start = incoming[0] / incoming[3]
    value_start = jnp.stack([incoming[1], incoming[2]], axis=1) / incoming[3][:, None, :]

    def sweep(carry, inputs):
        ratio_prev, value_prev = carry
        kappa_shell, source, shell_index = inputs
        lower, upper, diagonal = coefficients(kappa_shell, shell_index)
        pivot = diagonal - lower * ratio_prev
        ratio_now = upper / pivot
        value_now = (source - lower * value_prev) / pivot[:, None, :]
        return ((ratio_now, value_now), (ratio_now, value_now))

    _, (ratios, values) = lax.scan(
        sweep, (ratio_start, value_start), (diffusivity, right_side, global_shells)
    )

    def back_compose(carry, inputs):
        alpha, slope = carry
        ratio_now, value_now = inputs
        alpha = value_now - ratio_now[:, None, :] * alpha
        slope = -ratio_now * slope
        return ((alpha, slope), (alpha, slope))

    blank_value = jnp.zeros((ord_dev, halves, degrees), jnp.float32)
    unity = jnp.ones((ord_dev, degrees), jnp.float32)
    (alpha_dev, slope_dev), (alpha_all, slope_all) = lax.scan(
        back_compose, (blank_value, unity), (ratios, values), reverse=True
    )
    beyond, _ = prefix_2(
        (alpha_dev, slope_dev), "radial", combine_affine, (blank_value, unity), True
    )
    return alpha_all + slope_all[:, :, None, :] * beyond[None]


def solution(mesh):
    return jax.shard_map(
        on_device,
        mesh=mesh,
        in_specs=(
            P("radial", "mode", None, None),
            P("radial", "mode", None, None),
            P("mode", None, None),
            P("radial"),
        ),
        out_specs=P("radial", "mode", None, None),
        check_vma=False,
    )
```

profile of v0, /device:TPU:0, one launch (start us, length us, event | category | flops | bytes accessed | tf_op | source)
XLA Modules:
  0.0 700.0 jit_solution(18119201527040543334)
XLA Ops:
  8.5 5.2 fusion.40
  13.7 11.3 %copy.50 = bf16[32,16,2,768]{0,2,1,3:T(2,128)(2,1)} copy(bf16[32,16,2,768]{3,0,2,1:T(8,128)(2,1)S(1)} %fusion.40) | data formatting | bytes 3145728 | tf_op jit(solution)/shard_map/convert_element_type | solution.py:62
  25.0 8.3 %reshape.119 = bf16[4,2,98304]{2,1,0:T(2,128)(2,1)} reshape(bf16[768,16,2,32]{3,2,1,0:T(2,128)(2,1)} %bitcast.170) | data formatting | bytes 3145728
  33.3 6.5 all-to-all-start
  40.4 5.2 fusion.37
  45.6 11.3 %copy.54 = bf16[32,16,2,768]{0,2,1,3:T(2,128)(2,1)} copy(bf16[32,16,2,768]{3,0,2,1:T(8,128)(2,1)S(1)} %fusion.37) | data formatting | bytes 3145728 | tf_op jit(solution)/shard_map/convert_element_type | solution.py:68
  56.9 8.3 %reshape.121 = bf16[4,2,98304]{2,1,0:T(2,128)(2,1)} reshape(bf16[768,16,2,32]{3,2,1,0:T(2,128)(2,1)} %bitcast.171) | data formatting | bytes 3145728
  65.2 11.6 %all-to-all-done = bf16[4,2,98304]{2,1,0:T(2,128)(2,1)S(1)} async-done(((bf16[4,2,98304]{2,1,0:T(2,128)(2,1)}), bf16[4,2,98304]{2,1,0:T(2,128)(2,1)S(1)}, u32[]{:S(2)}, u32[]{:S(2)}) %all-to-all-start) | async-done | bytes 1572896 | tf_op jit(solution)/shard_map/all_to_all | solution.py:69
  82.9 4.7 reshape.120
  87.6 20.9 %copy.68 = bf16[32,16,2,4,192]{4,3,1,2,0:T(4,128)(2,1)} copy(bf16[32,16,2,4,192]{0,2,1,4,3:T(2,128)(2,1)} %bitcast.172) | data formatting | bytes 3145728 | tf_op jit(solution)/shard_map/all_to_all | solution.py:69
  110.5 7.2 %all-to-all-done.1 = bf16[4,2,98304]{2,1,0:T(2,128)(2,1)} async-done(((bf16[4,2,98304]{2,1,0:T(2,128)(2,1)}), bf16[4,2,98304]{2,1,0:T(2,128)(2,1)}, u32[]{:S(2)}, u32[]{:S(2)}) %all-to-all-start.1) | async-done | bytes 1572896 | tf_op jit(solution)/shard_map/all_to_all | solution.py:70
  117.7 6.4 reshape.122
  124.1 20.9 %copy.69 = bf16[32,16,2,4,192]{4,3,1,2,0:T(4,128)(2,1)} copy(bf16[32,16,2,4,192]{0,2,1,4,3:T(2,128)(2,1)} %bitcast.173) | data formatting | bytes 3145728 | tf_op jit(solution)/shard_map/all_to_all | solution.py:70
  148.4 14.8 %fusion.52 = f32[32,192,1536,1]{2,1,3,0:T(8,128)} fusion(bf16[32,64,2,192]{3,1,2,0:T(8,128)(2,1)S(1)} %bitcast.174, f32[64,1,1536]{2,0,1:T(8,128)S(1)} %get-tuple-element.644, f32[64,1,1536]{2,0,1:T(8,128)S(1)} %get-tuple-element.645), kind=kOutput, calls=%fused_computation.71 | convolution fusion | flops 2416508928 | bytes 40108032 | tf_op jit(solution)/shard_map/rmct,mcp->rtp/dot_general | solution.py:71
  163.1 17.3 %convert_bitcast_fusion = bf16[32,64,2,192]{3,1,0,2:T(8,128)(2,1)S(1)} fusion(f32[32,192,1536,1]{2,1,3,0:T(8,128)} %fusion.52, bf16[32,64,2,192]{3,1,2,0:T(8,128)(2,1)} %bitcast.179, f32[64,1,1536]{2,0,1:T(8,128)S(1)} %get-tuple-element.644, f32[64,1,1536]{2,0,1:T(8,128)S(1)} %get-tuple-element.645), kind=kOutput, calls=%fused_computation.54 | convolution fusion | flops 4852678656 | bytes 41680896 | tf_op jit(solution)/shard_map/rtp,mcp->rmct/dot_general | solution.py:78
  186.9 47.4 %all-to-all-done.2 = bf16[32,64,2,192]{3,0,2,1:T(8,128)(2,1)S(1)} async-done(((bf16[32,64,2,192]{3,0,2,1:T(8,128)(2,1)}), bf16[32,64,2,192]{3,0,2,1:T(8,128)(2,1)S(1)}, u32[]{:S(2)}, u32[]{:S(2)}) %all-to-all-start.2) | async-done | bytes 1572896 | tf_op jit(solution)/shard_map/all_to_all | solution.py:81
  242.1 7.6 %bitcast_add_fusion.1 = f32[32,16,2,384]{3,0,2,1:T(8,128)S(1)} fusion(f32[32,16,2,384]{3,2,1,0:T(2,128)} %param.14, bf16[32,16,2,768]{3,0,2,1:T(8,128)(2,1)} %all_to_all.50, bf16[16,384,768]{2,1,0:T(8,128)(2,1)} %param.16), kind=kOutput, calls=%fused_computation.57 | convolution fusion | flops 604372992 | bytes 14155776 | tf_op jit(solution)/shard_map/rmct,mjt->rmcj/dot_general | solution.py:82
  249.8 164.0 %while.77 = (s32[]{:T(128)}, f32[4,4,16,384]{3,2,1,0:T(8,128)S(1)}, s32[32]{0:T(128)S(1)}, f32[32]{0:T(128)S(1)}, f32[32,16,2,384]{3,0,2,1:T(8,128)S(1)}, /*inde...) while((s32[]{:T(128)}, f32[4,4,16,384]{3,2,1,0:T(8,128)S(1)}, ...), condition=%wide.region_2.3_spmd.clone, body=%wide.region_0.2_spmd.clone.sunk | while | flops 1161229 | bytes 2408801 | solution.py:120
  414.5 31.4 %all-gather.5.cloned.1.call-done = f32[32,4,16,384]{3,2,1,0:T(8,128)} async-done(((f32[4,4,16,384]{3,2,1,0:T(8,128)}), f32[32,4,16,384]{3,2,1,0:T(8,128)}) %all-gather.5.cloned.1.call-update) | async-done | bytes 3145744 | tf_op jit(solution)/shard_map/all_gather | solution.py:12
  446.0 9.0 %while.76 = (s32[]{:T(128)}, f32[4,4,16,384]{3,2,1,0:T(8,128)S(1)}, s32[]{:T(128)}, f32[8,4,4,16,384]{4,3,2,1,0:T(8,128)}, s32[]{:T(128)}) while((s32[]{:T(128)}, f32[4,4,16,384]{3,2,1,0:T(8,128)S(1)}, s32[]{:T(128)}, f32[8,4,4,16,384]{4,3,2,1,0:T(8,128)}, s32[]{:T(128)}) %tuple.172), condition=%wide.region_6.7_spmd, body=%wide.region_3.6_spmd.sunk | while | flops 1075203 | bytes 3588171 | solution.py:24
  457.4 185.0 %while.78 = (s32[]{:T(128)}, f32[16,384]{1,0:T(8,128)S(1)}, f32[16,2,384]{2,1,0:T(2,128)S(1)}, f32[32,16,384]{2,1,0:T(8,128)S(1)}, f32[32,16,2,384]{3,2,1,0:T(2,...) while((s32[]{:T(128)}, f32[16,384]{1,0:T(8,128)S(1)}, ...), condition=%wide.region_8.9_spmd.clone, body=%wide.region_7.8_spmd.clone.sunk | while | flops 92172 | bytes 419129 | solution.py:135
  643.1 29.2 %while.79 = (s32[]{:T(128)}, f32[16,2,384]{2,1,0:T(2,128)S(1)}, f32[16,384]{1,0:T(8,128)S(1)}, f32[32,16,2,384]{3,2,1,0:T(2,128)S(1)}, f32[32,16,384]{2,1,0:T(8,...) while((s32[]{:T(128)}, f32[16,2,384]{2,1,0:T(2,128)S(1)}, ...), condition=%wide.region_10.11_spmd.clone, body=%wide.region_9.10_spmd.clone.sunk | while | flops 55300 | bytes 344196 | solution.py:148
  672.4 9.5 %all-gather.1 = f32[128,2,384]{2,1,0:T(2,128)S(1)} all-gather(f32[16,2,384]{2,1,0:T(2,128)S(1)} %get-tuple-element.408), channel_id=3, replica_groups=mesh['radial'=8,'mode'=4] {'radial'}, dimensions={0}, use_global_device_ids=true | all-gather | bytes 442368 | tf_op jit(solution)/shard_map/all_gather | solution.py:12
  682.0 8.3 %all-gather.2 = f32[128,384]{1,0:T(8,128)S(1)} all-gather(f32[16,384]{1,0:T(8,128)S(1)} %get-tuple-element.409), channel_id=4, replica_groups=mesh['radial'=8,'mode'=4] {'radial'}, dimensions={0}, use_global_device_ids=true | all-gather | bytes 221184 | tf_op jit(solution)/shard_map/all_gather | solution.py:12
  (595 shorter events, 218.7 us)
Async XLA Ops:
  33.3 6.5 copy-start.2
  33.3 43.4 %all-to-all-start = ((bf16[4,2,98304]{2,1,0:T(2,128)(2,1)}), bf16[4,2,98304]{2,1,0:T(2,128)(2,1)S(1)}, u32[]{:S(2)}, u32[]{:S(2)}) async-start(bf16[4,2,98304]{2,1,0:T(2,128)(2,1)} %reshape.119), calls=%async_computation | async-start | bytes 3145728 | tf_op jit(solution)/shard_map/all_to_all | solution.py:69
  76.8 41.0 %all-to-all-start.1 = ((bf16[4,2,98304]{2,1,0:T(2,128)(2,1)}), bf16[4,2,98304]{2,1,0:T(2,128)(2,1)}, u32[]{:S(2)}, u32[]{:S(2)}) async-start(bf16[4,2,98304]{2,1,0:T(2,128)(2,1)} %reshape.121), calls=%async_computation.1 | async-start | bytes 3145728 | tf_op jit(solution)/shard_map/all_to_all | solution.py:70
  183.0 51.3 %all-to-all-start.2 = ((bf16[32,64,2,192]{3,0,2,1:T(8,128)(2,1)}), bf16[32,64,2,192]{3,0,2,1:T(8,128)(2,1)S(1)}, u32[]{:S(2)}, u32[]{:S(2)}) async-start(bf16[32,64,2,192]{3,0,2,1:T(8,128)(2,1)} %copy.57), calls=%async_computation.2 | async-start | bytes 4194304 | tf_op jit(solution)/shard_map/all_to_all | solution.py:81
  186.6 259.3 %all-gather.5.cloned.1.call-start = ((), (), s32[]{:S(2)}) async-start(), calls=%async_computation.3 | async-start | bytes 3538944 | tf_op jit(solution)/shard_map/all_gather | solution.py:12
  234.3 1.3 copy-start.1
  242.1 7.7 %copy-start.3 = (f32[32]{0:T(128)S(1)}, f32[32]{0:T(128)}, u32[]{:S(2)}) copy-start(f32[32]{0:T(128)} %param.17) | copy-start | bytes 388
  413.7 0.7 copy-start
Sparse Core Ops, SparseCore 0:
  414.6 31.2 all-gather.4
where the time goes:
time: 707 us; the launch traced here: 700 us
  loops' own time  204 us (29%)
  local copies, waits for them, and re-layouts  199 us (28%)
  other arithmetic  103 us (15%)
  waiting for transfers between devices  97.6 us (14%)
  matrix products  50.1 us (7%)
  blocking collectives  17.8 us (3%)
  starting transfers between devices  14.9 us (2%)
  between operations  13.7 us (2%)
    another operation x1, loops' own time, on_device(): lax.scan(sweep, (ratio_start, value_start), (diffusivity, right_side, glo...  102 us
    another operation x1, loops' own time, on_device(): lax.scan(compose, identity, (diffusivity, right_side, global_shells))  101 us
    dynamic_slice x224, local copies, waits for them, and re-layouts, on_device(): lax.scan(compose, identity, (diffusivity, right_side, global_shells))  79.9 us
    dynamic_update_slice x128, other arithmetic, on_device(): lax.scan(sweep, (ratio_start, value_start), (diffusivity, right_side, glo...  70.4 us
    all_to_all x1, waiting for transfers between devices, on_device(): lax.all_to_all(modes_grid, 'mode', split_axis=1, concat_axis=3, tiled=True)  47.4 us
    all_gather x1, waiting for transfers between devices, prefix_2(): pieces = jax.tree.map(lambda part: lax.all_gather(part, axis), value)  31.4 us
    unnamed x12, local copies, waits for them, and re-layouts  29.7 us
    all_to_all x2, local copies, waits for them, and re-layouts, on_device(): lax.all_to_all(flow_lat, 'mode', split_axis=3, concat_axis=1, tiled=True)  24.3 us
  transfers between devices with their start and end apart: 4, of which 4 were waited for; matrix products, arithmetic and copies ran while one was open for 8% of the time, Pallas kernels for 0%

commit v1 on v0

--- a/solution.py
+++ b/solution.py
@@ -66,7 +66,9 @@
         legendre,
         preferred_element_type=jnp.float32,
     ).astype(jnp.bfloat16)
-    field_piece = lax.all_to_all(field_lat, "mode", split_axis=3, concat_axis=1, tiled=True)
+    field_piece = jnp.concatenate(
+        lax.all_to_all(jnp.stack(jnp.split(field_lat, lax.psum(1, "mode"), 3)), "mode", 0, 0), 1
+    )
     flow_piece = lax.all_to_all(flow_lat, "mode", split_axis=3, concat_axis=1, tiled=True)
     field_grid = jnp.einsum(
         "rmct,mcp->rtp", field_piece, synth_table, preferred_element_type=jnp.float32

time: 707 us -> 698 us (0.987)
  local copies, waits for them, and re-layouts: 199 us -> 155 us
  waiting for transfers between devices: 97.6 us -> 123 us
    all_to_all x2 -> x0, local copies, waits for them, and re-layouts: 22.9 us -> none  [on_device(): lax.all_to_all(field_lat, 'mode', split_axis=3, concat_axis=1, tiled=True)]
    all_to_all x1, waiting for transfers between devices: 7.19 us -> 28.7 us  [on_device(): lax.all_to_all(flow_lat, 'mode', split_axis=3, concat_axis=1, tiled=True)]
    unnamed x12, local copies, waits for them, and re-layouts: 29.7 us -> 17.9 us
    convert_element_type x1 -> x0, local copies, waits for them, and re-layouts: 11.3 us -> none  [on_device(): field_lat = jnp.einsum('rmcj,mjt->rmct', scalar_field.astype(jnp.bfloat16...]
  transfers between devices with their start and end apart: 4 -> 4, of which waited for: 4 -> 4; matrix products, arithmetic and copies ran while one was open for 8% -> 6% of each run, Pallas kernels for 0% -> 0%
where the time goes in v1:
time: 698 us; the launch traced here: 692 us
  loops' own time  207 us (30%)
  local copies, waits for them, and re-layouts  155 us (22%)
  waiting for transfers between devices  123 us (18%)
  other arithmetic  109 us (16%)
  matrix products  51.7 us (7%)
  blocking collectives  17.8 us (3%)
  starting transfers between devices  14.1 us (2%)
  between operations  13.7 us (2%)
    another operation x1, loops' own time, on_device(): lax.scan(sweep, (ratio_start, value_start), (diffusivity, right_side, glo...  105 us
    another operation x1, loops' own time, on_device(): lax.scan(compose, identity, (diffusivity, right_side, global_shells))  101 us
    dynamic_slice x224, local copies, waits for them, and re-layouts, on_device(): lax.scan(compose, identity, (diffusivity, right_side, global_shells))  81.3 us
    dynamic_update_slice x128, other arithmetic, on_device(): lax.scan(sweep, (ratio_start, value_start), (diffusivity, right_side, glo...  75.1 us
    all_to_all x1, waiting for transfers between devices, on_device(): lax.all_to_all(modes_grid, 'mode', split_axis=1, concat_axis=3, tiled=True)  47.4 us
    all_gather x1, waiting for transfers between devices, prefix_2(): pieces = jax.tree.map(lambda part: lax.all_gather(part, axis), value)  31.4 us
    all_to_all x1, waiting for transfers between devices, on_device(): lax.all_to_all(flow_lat, 'mode', split_axis=3, concat_axis=1, tiled=True)  28.7 us
    all_to_all x2, local copies, waits for them, and re-layouts, on_device(): lax.all_to_all(flow_lat, 'mode', split_axis=3, concat_axis=1, tiled=True)  24.3 us
  transfers between devices with their start and end apart: 4, of which 4 were waited for; matrix products, arithmetic and copies ran while one was open for 6% of the time, Pallas kernels for 0%

profile of v1, /device:TPU:0, one launch (start us, length us, event | category | flops | bytes accessed | tf_op | source)
XLA Modules:
  0.0 691.5 jit_solution(11071039877651665291)
XLA Ops:
  8.5 5.2 fusion.39
  13.7 11.3 %copy.49 = bf16[32,16,2,768]{0,2,1,3:T(2,128)(2,1)} copy(bf16[32,16,2,768]{3,0,2,1:T(8,128)(2,1)S(1)} %fusion.39) | data formatting | bytes 3145728 | tf_op jit(solution)/shard_map/convert_element_type | solution.py:68
  25.0 8.3 %reshape.127 = bf16[4,2,98304]{2,1,0:T(2,128)(2,1)} reshape(bf16[768,16,2,32]{3,2,1,0:T(2,128)(2,1)} %bitcast.175) | data formatting | bytes 3145728
  33.3 6.5 all-to-all-start.1
  40.3 5.2 fusion.42
  48.0 28.7 %all-to-all-done.1 = bf16[4,2,98304]{2,1,0:T(2,128)(2,1)S(1)} async-done(((bf16[4,2,98304]{2,1,0:T(2,128)(2,1)}), bf16[4,2,98304]{2,1,0:T(2,128)(2,1)S(1)}, u32[]{:S(2)}, u32[]{:S(2)}) %all-to-all-start.1) | async-done | bytes 1572896 | tf_op jit(solution)/shard_map/all_to_all | solution.py:72
  77.9 3.8 all-to-all-start
  83.3 6.4 reshape.128
  89.7 20.9 %copy.63 = bf16[32,16,2,4,192]{4,3,1,2,0:T(4,128)(2,1)} copy(bf16[32,16,2,4,192]{0,2,1,4,3:T(2,128)(2,1)} %bitcast.176) | data formatting | bytes 3145728 | tf_op jit(solution)/shard_map/all_to_all | solution.py:72
  110.6 3.4 copy.51
  113.9 15.3 %all-to-all-done = bf16[4,32,16,2,192]{4,1,3,2,0:T(8,128)(2,1)S(1)} async-done(((bf16[4,32,16,2,192]{4,1,3,2,0:T(8,128)(2,1)}), bf16[4,32,16,2,192]{4,1,3,2,0:T(8,128)(2,1)S(1)}, u32[]{:S(2)}, u32[]{:S(2)}) %all-to-all-start) | async-done | bytes 1572896 | tf_op jit(solution)/shard_map/all_to_all | solution.py:70
  129.2 16.4 %fusion.27 = f32[32,192,1536,1]{2,1,3,0:T(8,128)} fusion(bf16[32,64,2,192]{3,0,2,1:T(8,128)(2,1)S(1)} %bitcast.177, f32[64,1,1536]{2,0,1:T(8,128)S(1)} %get-tuple-element.648, f32[64,1,1536]{2,0,1:T(8,128)S(1)} %get-tuple-element.649), kind=kOutput, calls=%fused_computation.55 | convolution fusion | flops 2416508928 | bytes 40108032 | tf_op jit(solution)/shard_map/rmct,mcp->rtp/dot_general | solution.py:73
  145.7 17.3 %convert_bitcast_fusion = bf16[32,64,2,192]{3,1,0,2:T(8,128)(2,1)S(1)} fusion(f32[32,192,1536,1]{2,1,3,0:T(8,128)} %fusion.27, bf16[32,64,2,192]{3,1,2,0:T(8,128)(2,1)} %bitcast.181, f32[64,1,1536]{2,0,1:T(8,128)S(1)} %get-tuple-element.648, f32[64,1,1536]{2,0,1:T(8,128)S(1)} %get-tuple-element.649), kind=kOutput, calls=%fused_computation.57 | convolution fusion | flops 4852678656 | bytes 41680896 | tf_op jit(solution)/shard_map/rtp,mcp->rmct/dot_general | solution.py:80
  165.5 3.6 all-to-all-start.2
  169.5 47.4 %all-to-all-done.2 = bf16[32,64,2,192]{3,0,2,1:T(8,128)(2,1)S(1)} async-done(((bf16[32,64,2,192]{3,0,2,1:T(8,128)(2,1)}), bf16[32,64,2,192]{3,0,2,1:T(8,128)(2,1)S(1)}, u32[]{:S(2)}, u32[]{:S(2)}) %all-to-all-start.2) | async-done | bytes 1572896 | tf_op jit(solution)/shard_map/all_to_all | solution.py:83
  218.2 3.6 copy.82
  224.6 7.6 %bitcast_add_fusion.1 = f32[32,16,2,384]{3,0,2,1:T(8,128)S(1)} fusion(f32[32,16,2,384]{3,2,1,0:T(2,128)} %param.14, bf16[32,16,2,768]{3,0,2,1:T(8,128)(2,1)} %all_to_all.37, bf16[16,384,768]{2,1,0:T(8,128)(2,1)} %param.16), kind=kOutput, calls=%fused_computation.60 | convolution fusion | flops 604372992 | bytes 14155776 | tf_op jit(solution)/shard_map/rmct,mjt->rmcj/dot_general | solution.py:84
  232.3 164.2 %while.77 = (s32[]{:T(128)}, f32[4,4,16,384]{3,2,1,0:T(8,128)S(1)}, s32[32]{0:T(128)S(1)}, f32[32]{0:T(128)S(1)}, f32[32,16,2,384]{3,0,2,1:T(8,128)S(1)}, /*inde...) while((s32[]{:T(128)}, f32[4,4,16,384]{3,2,1,0:T(8,128)S(1)}, ...), condition=%wide.region_2.3_spmd.clone, body=%wide.region_0.2_spmd.clone.sunk | while | flops 1161229 | bytes 2408801 | solution.py:122
  397.3 31.4 %all-gather.5.cloned.1.call-done = f32[32,4,16,384]{3,2,1,0:T(8,128)} async-done(((f32[4,4,16,384]{3,2,1,0:T(8,128)}), f32[32,4,16,384]{3,2,1,0:T(8,128)}) %all-gather.5.cloned.1.call-update) | async-done | bytes 3145744 | tf_op jit(solution)/shard_map/all_gather | solution.py:12
  428.8 9.0 %while.76 = (s32[]{:T(128)}, f32[4,4,16,384]{3,2,1,0:T(8,128)S(1)}, s32[]{:T(128)}, f32[8,4,4,16,384]{4,3,2,1,0:T(8,128)}, s32[]{:T(128)}) while((s32[]{:T(128)}, f32[4,4,16,384]{3,2,1,0:T(8,128)S(1)}, s32[]{:T(128)}, f32[8,4,4,16,384]{4,3,2,1,0:T(8,128)}, s32[]{:T(128)}) %tuple.175), condition=%wide.region_6.7_spmd, body=%wide.region_3.6_spmd.sunk | while | flops 1075203 | bytes 3588171 | solution.py:24
  440.1 193.8 %while.78 = (s32[]{:T(128)}, f32[16,384]{1,0:T(8,128)S(1)}, f32[16,2,384]{2,1,0:T(2,128)S(1)}, f32[32,16,384]{2,1,0:T(8,128)S(1)}, f32[32,16,2,384]{3,2,1,0:T(2,...) while((s32[]{:T(128)}, f32[16,384]{1,0:T(8,128)S(1)}, ...), condition=%wide.region_8.9_spmd.clone, body=%wide.region_7.8_spmd.clone.sunk | while | flops 92172 | bytes 419129 | solution.py:137
  634.7 29.2 %while.79 = (s32[]{:T(128)}, f32[16,2,384]{2,1,0:T(2,128)S(1)}, f32[16,384]{1,0:T(8,128)S(1)}, f32[32,16,2,384]{3,2,1,0:T(2,128)S(1)}, f32[32,16,384]{2,1,0:T(8,...) while((s32[]{:T(128)}, f32[16,2,384]{2,1,0:T(2,128)S(1)}, ...), condition=%wide.region_10.11_spmd.clone, body=%wide.region_9.10_spmd.clone.sunk | while | flops 55300 | bytes 344196 | solution.py:150
  663.9 9.5 %all-gather.1 = f32[128,2,384]{2,1,0:T(2,128)S(1)} all-gather(f32[16,2,384]{2,1,0:T(2,128)S(1)} %get-tuple-element.408), channel_id=3, replica_groups=mesh['radial'=8,'mode'=4] {'radial'}, dimensions={0}, use_global_device_ids=true | all-gather | bytes 442368 | tf_op jit(solution)/shard_map/all_gather | solution.py:12
  673.5 8.3 %all-gather.2 = f32[128,384]{1,0:T(8,128)S(1)} all-gather(f32[16,384]{1,0:T(8,128)S(1)} %get-tuple-element.409), channel_id=4, replica_groups=mesh['radial'=8,'mode'=4] {'radial'}, dimensions={0}, use_global_device_ids=true | all-gather | bytes 221184 | tf_op jit(solution)/shard_map/all_gather | solution.py:12
  (594 shorter events, 211.3 us)
Async XLA Ops:
  33.3 6.5 copy-start.2
  33.3 43.4 %all-to-all-start.1 = ((bf16[4,2,98304]{2,1,0:T(2,128)(2,1)}), bf16[4,2,98304]{2,1,0:T(2,128)(2,1)S(1)}, u32[]{:S(2)}, u32[]{:S(2)}) async-start(bf16[4,2,98304]{2,1,0:T(2,128)(2,1)} %reshape.127), calls=%async_computation.1 | async-start | bytes 3145728 | tf_op jit(solution)/shard_map/all_to_all | solution.py:72
  76.8 1.1 copy-start.3
  77.9 51.3 %all-to-all-start = ((bf16[4,32,16,2,192]{4,1,3,2,0:T(8,128)(2,1)}), bf16[4,32,16,2,192]{4,1,3,2,0:T(8,128)(2,1)S(1)}, u32[]{:S(2)}, u32[]{:S(2)}) async-start(bf16[4,32,16,2,192]{4,1,3,2,0:T(8,128)(2,1)} %pad_maximum_fusion.1), calls=%async_computation | async-start | bytes 4194304 | tf_op jit(solution)/shard_map/all_to_all | solution.py:70
  165.5 51.3 %all-to-all-start.2 = ((bf16[32,64,2,192]{3,0,2,1:T(8,128)(2,1)}), bf16[32,64,2,192]{3,0,2,1:T(8,128)(2,1)S(1)}, u32[]{:S(2)}, u32[]{:S(2)}) async-start(bf16[32,64,2,192]{3,0,2,1:T(8,128)(2,1)} %copy.52), calls=%async_computation.2 | async-start | bytes 4194304 | tf_op jit(solution)/shard_map/all_to_all | solution.py:83
  169.1 259.6 %all-gather.5.cloned.1.call-start = ((), (), s32[]{:S(2)}) async-start(), calls=%async_computation.3 | async-start | bytes 3538944 | tf_op jit(solution)/shard_map/all_gather | solution.py:12
  216.9 1.3 copy-start.1
  224.6 7.7 %copy-start.4 = (f32[32]{0:T(128)S(1)}, f32[32]{0:T(128)}, u32[]{:S(2)}) copy-start(f32[32]{0:T(128)} %param.17) | copy-start | bytes 388
  396.5 0.7 copy-start
Sparse Core Ops, SparseCore 0:
  397.4 31.2 all-gather.4
